TPU v7x, 32 devices: a whole 2x2x4 slice. The times are simulated.
32 devices in a mesh: dp: 8 (over z, y), mp: 4 (over x, core).
Axes of the slice: x: 2, y: 2, z: 4, core: 2. Of those that a mesh axis runs over, the one named last changes fastest.
Arguments:
- tokens: bfloat16 [8192, 2048], P('dp'), may hold values from -6 to 6
- out_cot: bfloat16 [8192, 2048], P('dp'), may hold values from -23 to 23
- lengths: int32 [8], P('dp'), may hold values from 1 to 1024, 6144 in all
- seq_family: int32 [8, 1], P('dp'), may hold values from 0 to 3
- family_tokens: int32 [4], replicated, may hold values from 100000 to 3999999
- norm_master: float32 [2048, 6], P('dp'), may hold values from -0.5 to 2.4, as said below
- attn_bias_master: float32 [2, 2048], P(None, 'mp'), may hold values from -2 to 2
- qkv_master: float32 [2048, 3, 2048], P('dp', None, 'mp'), may hold values from -0.125 to 0.125
- proj_master: float32 [2048, 2048], P('dp', 'mp'), may hold values from -1.5 to 1.5
- fc_bias_master: float32 [8192], P('mp'), may hold values from -1.5 to 1.5
- fc_master: float32 [2048, 8192], P('dp', 'mp'), may hold values from -0.125 to 0.125
- down_master: float32 [2048, 8192], P('dp', 'mp'), may hold values from -0.0625 to 0.0625
- norm_moment: float32 [2048, 6], P('dp'), may hold values from -0.0008544922 to 0.0008544922
- attn_bias_moment: float32 [2, 2048], P(None, 'mp'), may hold values from -0.0008544922 to 0.0008544922
- qkv_moment: float32 [2048, 3, 2048], P('dp', None, 'mp'), may hold values from -0.0008544922 to 0.0008544922
- proj_moment: float32 [2048, 2048], P('dp', 'mp'), may hold values from -0.0008544922 to 0.0008544922
- fc_bias_moment: float32 [8192], P('mp'), may hold values from -0.0008544922 to 0.0008544922
- fc_moment: float32 [2048, 8192], P('dp', 'mp'), may hold values from -0.0008544922 to 0.0008544922
- down_moment: float32 [2048, 8192], P('dp', 'mp'), may hold values from -0.0008544922 to 0.0008544922
- norm_average: float32 [2048, 6], P('dp'), may hold values from 0.5 to 1.5
- attn_bias_average: float32 [2, 2048], P(None, 'mp'), may hold values from -2 to 2
- qkv_average: float32 [2048, 3, 2048], P('dp', None, 'mp'), may hold values from -0.125 to 0.125
- proj_average: float32 [2048, 2048], P('dp', 'mp'), may hold values from -1.5 to 1.5
- fc_bias_average: float32 [8192], P('mp'), may hold values from -1.5 to 1.5
- fc_average: float32 [2048, 8192], P('dp', 'mp'), may hold values from -0.125 to 0.125
- down_average: float32 [2048, 8192], P('dp', 'mp'), may hold values from -0.0625 to 0.0625
Outputs:
- block_out: bfloat16 [8192, 2048], P('dp')
- input_grad: float32 [8192, 2048], P('dp')
- norm_grad: float32 [2048, 6], P('dp')
- attn_bias_grad: float32 [2, 2048], P(None, 'mp')
- qkv_grad: float32 [2048, 3, 2048], P('dp', None, 'mp')
- proj_grad: float32 [2048, 2048], P('dp', 'mp')
- fc_bias_grad: float32 [8192], P('mp')
- fc_grad: float32 [2048, 8192], P('dp', 'mp')
- down_grad: float32 [2048, 8192], P('dp', 'mp')
- norm_momentum: float32 [2048, 6], P('dp')
- attn_bias_momentum: float32 [2, 2048], P(None, 'mp')
- qkv_momentum: float32 [2048, 3, 2048], P('dp', None, 'mp')
- proj_momentum: float32 [2048, 2048], P('dp', 'mp')
- fc_bias_momentum: float32 [8192], P('mp')
- fc_momentum: float32 [2048, 8192], P('dp', 'mp')
- down_momentum: float32 [2048, 8192], P('dp', 'mp')
- norm_averaged: float32 [2048, 6], P('dp')
- attn_bias_averaged: float32 [2, 2048], P(None, 'mp')
- qkv_averaged: float32 [2048, 3, 2048], P('dp', None, 'mp')
- proj_averaged: float32 [2048, 2048], P('dp', 'mp')
- fc_bias_averaged: float32 [8192], P('mp')
- fc_averaged: float32 [2048, 8192], P('dp', 'mp')
- down_averaged: float32 [2048, 8192], P('dp', 'mp')
- norm_updated: float32 [2048, 6], P('dp')
- attn_bias_updated: float32 [2, 2048], P(None, 'mp')
- qkv_updated: float32 [2048, 3, 2048], P('dp', None, 'mp')
- proj_updated: float32 [2048, 2048], P('dp', 'mp')
- fc_bias_updated: float32 [8192], P('mp')
- fc_updated: float32 [2048, 8192], P('dp', 'mp')
- down_updated: float32 [2048, 8192], P('dp', 'mp')
- norm_copy: bfloat16 [2048, 6], P('dp')
- attn_bias_copy: bfloat16 [2, 2048], P(None, 'mp')
- qkv_copy: bfloat16 [2048, 3, 2048], P('dp', None, 'mp')
- proj_copy: bfloat16 [2048, 2048], P('dp', 'mp')
- fc_bias_copy: bfloat16 [8192], P('mp')
- fc_copy: bfloat16 [2048, 8192], P('dp', 'mp')
- down_copy: bfloat16 [2048, 8192], P('dp', 'mp')
- grad_norm: float32 [], replicated
Inputs may be any that keep to these rules, and one draw needn't show every extreme that they name: `lengths`: they sum to 6144; the longest is 1024. `seq_family`: every family has a sequence. `norm_master`: gains positive, biases of either sign.
All inputs are finite; a program needn't handle non-finite values. No bound on the sum of `lengths` on one device may be relied on, other than what follows from the above.
Results may differ from a plain program's by a relative error of at most 0.012.
The roundings to bfloat16 on the way count: a program that leaves them out, or rounds other values in their place, can miss the bound.
Values may be sent and summed in bfloat16 or wider, within the bound.
A program may use at most 256 MiB of HBM per device.

v0:
```python
import math
import jax
import jax.numpy as jnp
from jax import lax
from jax.sharding import PartitionSpec as P

HEAD_DIM = 128
LEN = 1024
EPS = 1e-05
MOMENTUM = 0.9
RATE = 192.0
KEEP = 0.9
NEG = -1e30


def layer_norm(value, gain, shift):
    centre = jnp.mean(value, axis=-1, keepdims=True)
    centred = value - centre
    spread = jnp.mean(centred * centred, axis=-1, keepdims=True)
    return centred * lax.rsqrt(spread + EPS) * gain + shift


def gelu_tanh(value):
    return (
        0.5
        * value
        * (1.0 + jnp.tanh(0.7978845608028654 * (value + 0.044715 * value * value * value)))
    )


def local(
    tokens,
    out_cot,
    lengths,
    seq_family,
    family_tokens,
    norm_master,
    attn_bias_master,
    qkv_master,
    proj_master,
    fc_bias_master,
    fc_master,
    down_master,
    norm_moment,
    attn_bias_moment,
    qkv_moment,
    proj_moment,
    fc_bias_moment,
    fc_moment,
    down_moment,
    norm_average,
    attn_bias_average,
    qkv_average,
    proj_average,
    fc_bias_average,
    fc_average,
    down_average,
):
    seq_count = lengths.shape[0]
    row_count = tokens.shape[0]
    seq_len = row_count // seq_count
    family_count = family_tokens.shape[0]
    local_heads = qkv_master.shape[2] // HEAD_DIM
    head_width = qkv_master.shape[2]
    scale = 1.0 / math.sqrt(HEAD_DIM)
    mp_count = lax.axis_size("mp")
    dp_count = lax.axis_size("dp")

    def sum_over_mp(term_fn):
        summed = lax.psum(term_fn(0, row_count), "mp")
        return summed

    family_ids = jnp.arange(family_count, dtype=jnp.int32)
    member = seq_family == family_ids[None, :]
    local_counts = jnp.sum(jnp.where(member, lengths[:, None], 0), axis=0).astype(jnp.float32)
    counts = lax.psum(local_counts, "dp")
    valid_total = jnp.sum(counts)
    share = family_tokens.astype(jnp.float32) / jnp.sum(family_tokens).astype(jnp.float32)
    family_weight = share * valid_total / jnp.maximum(counts, float(LEN // 2))
    seq_weight = jnp.sum(jnp.where(member, family_weight[None, :], 0.0), axis=1)
    places = jnp.arange(seq_len, dtype=jnp.int32)
    token_weight = jnp.where(places[None, :] < lengths[:, None], seq_weight[:, None], 0.0).reshape(
        row_count
    )
    causal = places[:, None] >= places[None, :]
    low_norm = norm_master.astype(jnp.bfloat16)
    low_qkv = qkv_master.astype(jnp.bfloat16)
    low_proj = proj_master.astype(jnp.bfloat16)
    low_fc = fc_master.astype(jnp.bfloat16)
    low_down = down_master.astype(jnp.bfloat16)
    w_qkv, w_proj, w_fc, w_down, w_norm = (
        lax.all_gather(low_qkv, "dp", axis=0, tiled=True),
        lax.all_gather(low_proj, "dp", axis=0, tiled=True),
        lax.all_gather(low_fc, "dp", axis=0, tiled=True),
        lax.all_gather(low_down, "dp", axis=0, tiled=True),
        lax.all_gather(low_norm, "dp", axis=0, tiled=True),
    )
    norm_full = w_norm.astype(jnp.float32)
    bias_rows = jnp.stack(
        [attn_bias_master[0], jnp.zeros_like(attn_bias_master[0]), attn_bias_master[1]], axis=0
    )
    x_in = tokens.astype(jnp.float32)
    ln1_low = layer_norm(x_in, norm_full[:, 0], norm_full[:, 1]).astype(jnp.bfloat16)
    qkv = (
        jnp.einsum("td,dce->tce", ln1_low, w_qkv, preferred_element_type=jnp.float32)
        + bias_rows[None]
    )
    qkv = qkv.astype(jnp.bfloat16)
    heads = qkv.reshape(seq_count, seq_len, 3, local_heads, HEAD_DIM)

    def attend(one_seq):
        query_rows = one_seq[:, 0]
        key_rows = one_seq[:, 1]
        value_rows = one_seq[:, 2]
        scores = (
            jnp.einsum("qhd,khd->hqk", query_rows, key_rows, preferred_element_type=jnp.float32)
            * scale
        )
        scores = jnp.where(causal[None], scores, NEG)
        row_top = jnp.max(scores, axis=-1, keepdims=True)
        log_total = row_top + jnp.log(jnp.sum(jnp.exp(scores - row_top), axis=-1, keepdims=True))
        attn_prob = jnp.exp(scores - log_total).astype(jnp.bfloat16)
        mixed = jnp.einsum(
            "hqk,khd->qhd", attn_prob, value_rows, preferred_element_type=jnp.float32
        )
        return (mixed.astype(jnp.bfloat16), log_total)

    mixed_low, log_kept = lax.map(attend, heads)
    mixed_low = mixed_low.reshape(row_count, head_width)

    def attn_term(start, count):
        return jnp.einsum("te,de->td", mixed_low, w_proj, preferred_element_type=jnp.float32)

    residual_part = x_in + sum_over_mp(attn_term) + norm_full[:, 4]
    ln2_part, ln2_back = jax.vjp(layer_norm, residual_part, norm_full[:, 2], norm_full[:, 3])
    ln2_low = ln2_part.astype(jnp.bfloat16)
    pre_act = (
        jnp.einsum("td,df->tf", ln2_low, w_fc, preferred_element_type=jnp.float32)
        + fc_bias_master[None]
    )
    hidden_act, gelu_back = jax.vjp(gelu_tanh, pre_act)
    hidden_low = hidden_act.astype(jnp.bfloat16)

    def mlp_term(start, count):
        return jnp.einsum("tf,df->td", hidden_low, w_down, preferred_element_type=jnp.float32)

    block_part = (residual_part + sum_over_mp(mlp_term) + norm_full[:, 5]).astype(jnp.bfloat16)
    upstream = token_weight[:, None] * out_cot.astype(jnp.float32)
    upstream_low = upstream.astype(jnp.bfloat16)
    down_sum = jnp.einsum("td,tf->df", upstream_low, hidden_low, preferred_element_type=jnp.float32)
    back_act = jnp.einsum("td,df->tf", upstream_low, w_down, preferred_element_type=jnp.float32)
    back_pre = gelu_back(back_act)[0].astype(jnp.bfloat16)
    fc_bias_sum = jnp.sum(back_pre, axis=0, dtype=jnp.float32)
    fc_sum = jnp.einsum("td,tf->df", ln2_low, back_pre, preferred_element_type=jnp.float32)

    def fc_back_term(start, count):
        return jnp.einsum("tf,df->td", back_pre, w_fc, preferred_element_type=jnp.float32)

    back_ln2 = sum_over_mp(fc_back_term)
    back_resid_part, gain2_sum, shift2_sum = ln2_back(back_ln2)
    back_resid_part = upstream + back_resid_part
    back_attn_low = back_resid_part.astype(jnp.bfloat16)
    proj_sum = jnp.einsum("td,te->de", back_attn_low, mixed_low, preferred_element_type=jnp.float32)
    back_mixed = jnp.einsum(
        "td,de->te", back_attn_low, w_proj, preferred_element_type=jnp.float32
    ).astype(jnp.bfloat16)
    back_mixed = back_mixed.reshape(seq_count, seq_len, local_heads, HEAD_DIM)

    def attend_back(items):
        one_seq, log_total, back_seq = items
        query_rows = one_seq[:, 0]
        key_rows = one_seq[:, 1]
        value_rows = one_seq[:, 2]
        scores = (
            jnp.einsum("qhd,khd->hqk", query_rows, key_rows, preferred_element_type=jnp.float32)
            * scale
        )
        scores = jnp.where(causal[None], scores, NEG)
        attn_prob = jnp.exp(scores - log_total)
        prob_low = attn_prob.astype(jnp.bfloat16)
        back_value = jnp.einsum(
            "hqk,qhd->khd", prob_low, back_seq, preferred_element_type=jnp.float32
        )
        back_prob = jnp.einsum(
            "qhd,khd->hqk", back_seq, value_rows, preferred_element_type=jnp.float32
        )
        back_score = attn_prob * (
            back_prob - jnp.sum(attn_prob * back_prob, axis=-1, keepdims=True)
        )
        back_score = back_score.astype(jnp.bfloat16)
        back_query = (
            jnp.einsum("hqk,khd->qhd", back_score, key_rows, preferred_element_type=jnp.float32)
            * scale
        )
        back_key = (
            jnp.einsum("hqk,qhd->khd", back_score, query_rows, preferred_element_type=jnp.float32)
            * scale
        )
        return jnp.stack([back_query, back_key, back_value], axis=1).astype(jnp.bfloat16)

    back_heads = lax.map(attend_back, (heads, log_kept, back_mixed))
    back_qkv = back_heads.reshape(row_count, 3, head_width)
    attn_bias_sum = jnp.sum(back_qkv[:, 0::2], axis=0, dtype=jnp.float32)
    qkv_sum = jnp.einsum("td,tce->dce", ln1_low, back_qkv, preferred_element_type=jnp.float32)

    def qkv_back_term(start, count):
        return jnp.einsum("tce,dce->td", back_qkv, w_qkv, preferred_element_type=jnp.float32)

    back_ln1 = sum_over_mp(qkv_back_term)
    ln1_again, ln1_back = jax.vjp(layer_norm, x_in, norm_full[:, 0], norm_full[:, 1])
    back_input, gain1_sum, shift1_sum = ln1_back(back_ln1)
    whole = back_resid_part + back_input
    norm_part = jnp.stack(
        [
            gain1_sum,
            shift1_sum,
            gain2_sum,
            shift2_sum,
            jnp.sum(back_resid_part, axis=0),
            jnp.sum(upstream, axis=0),
        ],
        axis=1,
    )
    qkv_reduced, proj_reduced, fc_reduced, down_reduced, norm_reduced = (
        lax.psum_scatter(qkv_sum, "dp", scatter_dimension=0, tiled=True),
        lax.psum_scatter(proj_sum, "dp", scatter_dimension=0, tiled=True),
        lax.psum_scatter(fc_sum, "dp", scatter_dimension=0, tiled=True),
        lax.psum_scatter(down_sum, "dp", scatter_dimension=0, tiled=True),
        lax.psum_scatter(norm_part, "dp", scatter_dimension=0, tiled=True),
    )
    attn_bias_reduced, fc_bias_reduced = lax.psum((attn_bias_sum, fc_bias_sum), "dp")
    raw_grads = [
        reduced / valid_total
        for reduced in (
            norm_reduced,
            attn_bias_reduced,
            qkv_reduced,
            proj_reduced,
            fc_bias_reduced,
            fc_reduced,
            down_reduced,
        )
    ]
    local_squares = jnp.sum(raw_grads[0] * raw_grads[0]) / float(mp_count)
    local_squares = local_squares + jnp.sum(raw_grads[1] * raw_grads[1]) / float(dp_count)
    local_squares = local_squares + jnp.sum(raw_grads[4] * raw_grads[4]) / float(dp_count)
    for grad_raw in (raw_grads[2], raw_grads[3], raw_grads[5], raw_grads[6]):
        local_squares = local_squares + jnp.sum(grad_raw * grad_raw)
    squares = lax.psum(local_squares, ("dp", "mp"))
    grad_norm = jnp.sqrt(squares)
    clip_factor = jnp.minimum(1.0, 1.0 / (grad_norm + 1e-06))
    masters = (
        norm_master,
        attn_bias_master,
        qkv_master,
        proj_master,
        fc_bias_master,
        fc_master,
        down_master,
    )
    moments = (
        norm_moment,
        attn_bias_moment,
        qkv_moment,
        proj_moment,
        fc_bias_moment,
        fc_moment,
        down_moment,
    )
    averages = (
        norm_average,
        attn_bias_average,
        qkv_average,
        proj_average,
        fc_bias_average,
        fc_average,
        down_average,
    )
    grads_out = []
    momenta_out = []
    averaged_out = []
    updated_out = []
    copies_out = []
    for master, moment, average, grad_raw in zip(masters, moments, averages, raw_grads):
        clipped = grad_raw * clip_factor
        momentum = MOMENTUM * moment + clipped
        updated = master - RATE * (clipped + MOMENTUM * momentum)
        averaged = KEEP * average + (1.0 - KEEP) * updated
        grads_out.append(clipped)
        momenta_out.append(momentum)
        averaged_out.append(averaged)
        updated_out.append(updated)
        copies_out.append(updated.astype(jnp.bfloat16))
    return (
        block_part,
        whole,
        grads_out[0],
        grads_out[1],
        grads_out[2],
        grads_out[3],
        grads_out[4],
        grads_out[5],
        grads_out[6],
        momenta_out[0],
        momenta_out[1],
        momenta_out[2],
        momenta_out[3],
        momenta_out[4],
        momenta_out[5],
        momenta_out[6],
        averaged_out[0],
        averaged_out[1],
        averaged_out[2],
        averaged_out[3],
        averaged_out[4],
        averaged_out[5],
        averaged_out[6],
        updated_out[0],
        updated_out[1],
        updated_out[2],
        updated_out[3],
        updated_out[4],
        updated_out[5],
        updated_out[6],
        copies_out[0],
        copies_out[1],
        copies_out[2],
        copies_out[3],
        copies_out[4],
        copies_out[5],
        copies_out[6],
        grad_norm,
    )


def solution(mesh):
    placed = (
        P("dp", None),
        P("dp", None),
        P("dp"),
        P("dp", None),
        P(),
        P("dp", None),
        P(None, "mp"),
        P("dp", None, "mp"),
        P("dp", "mp"),
        P("mp"),
        P("dp", "mp"),
        P("dp", "mp"),
        P("dp", None),
        P(None, "mp"),
        P("dp", None, "mp"),
        P("dp", "mp"),
        P("mp"),
        P("dp", "mp"),
        P("dp", "mp"),
        P("dp", None),
        P(None, "mp"),
        P("dp", None, "mp"),
        P("dp", "mp"),
        P("mp"),
        P("dp", "mp"),
        P("dp", "mp"),
    )
    return jax.shard_map(
        local,
        mesh=mesh,
        in_specs=placed,
        out_specs=(
            P("dp", None),
            P("dp", None),
            P("dp", None),
            P(None, "mp"),
            P("dp", None, "mp"),
            P("dp", "mp"),
            P("mp"),
            P("dp", "mp"),
            P("dp", "mp"),
            P("dp", None),
            P(None, "mp"),
            P("dp", None, "mp"),
            P("dp", "mp"),
            P("mp"),
            P("dp", "mp"),
            P("dp", "mp"),
            P("dp", None),
            P(None, "mp"),
            P("dp", None, "mp"),
            P("dp", "mp"),
            P("mp"),
            P("dp", "mp"),
            P("dp", "mp"),
            P("dp", None),
            P(None, "mp"),
            P("dp", None, "mp"),
            P("dp", "mp"),
            P("mp"),
            P("dp", "mp"),
            P("dp", "mp"),
            P("dp", None),
            P(None, "mp"),
            P("dp", None, "mp"),
            P("dp", "mp"),
            P("mp"),
            P("dp", "mp"),
            P("dp", "mp"),
            P(),
        ),
        check_vma=False,
    )
```

profile of v0, /device:TPU:0, one launch (start us, length us, event | category | flops | bytes accessed | tf_op | source)
XLA Modules:
  0.0 2152.3 jit_solution(12280135592228971859)
XLA Ops:
  19.1 32.9 %all_gather.15 = bf16[2048,6]{0,1:T(8,128)(2,1)S(1)} all-gather(bf16[256,6]{0,1:T(8,128)(2,1)S(1)} %convert_element_type.108), channel_id=1, replica_groups=mesh['dp'=8,'mp'=4] {'dp'}, dimensions={0}, use_global_device_ids=true | all-gather | bytes 27648 | tf_op jit(solution)/shard_map/all_gather | solution.py:96
  52.7 61.0 %all-gather.5.cloned.1.call-done = bf16[2048,3,512]{0,2,1:T(8,128)(2,1)} async-done(((bf16[256,3,512]{0,2,1:T(8,128)(2,1)}), bf16[2048,3,512]{0,2,1:T(8,128)(2,1)}) %all-gather.5.cloned.1.call-update) | async-done | bytes 6291472 | tf_op jit(solution)/shard_map/all_gather | solution.py:92
  113.7 11.1 add_convert_fusion.2
  140.5 23.5 %all-gather.7.cloned.1.call-done = bf16[2048,512]{1,0:T(8,128)(2,1)} async-done(((bf16[256,512]{1,0:T(8,128)(2,1)}), bf16[2048,512]{1,0:T(8,128)(2,1)}) %all-gather.7.cloned.1.call-update) | async-done | bytes 2097168 | tf_op jit(solution)/shard_map/all_gather | solution.py:93
  178.8 18.5 psum.58
  201.1 121.8 %all-reduce.6.cloned.1.call-done = f32[1024,2048]{1,0:T(8,128)} async-done(((f32[1024,2048]{1,0:T(8,128)}), f32[1024,2048]{1,0:T(8,128)}) %all-reduce.6.cloned.1.call-update) | async-done | bytes 8388624 | tf_op jit(solution)/shard_map/psum | solution.py:70
  333.0 117.6 %all-gather.9.cloned.1.call-done = bf16[2048,2048]{1,0:T(8,128)(2,1)} async-done(((bf16[256,2048]{1,0:T(8,128)(2,1)}), bf16[2048,2048]{1,0:T(8,128)(2,1)}) %all-gather.9.cloned.1.call-update) | async-done | bytes 8388624 | tf_op jit(solution)/shard_map/all_gather | solution.py:94
  450.6 15.9 fusion.51
  466.5 109.8 %all-gather.11.cloned.1.call-done = bf16[2048,2048]{1,0:T(8,128)(2,1)} async-done(((bf16[256,2048]{1,0:T(8,128)(2,1)}), bf16[2048,2048]{1,0:T(8,128)(2,1)}) %all-gather.11.cloned.1.call-update) | async-done | bytes 8388624 | tf_op jit(solution)/shard_map/all_gather | solution.py:95
  576.3 21.0 convert_reduce_fusion.1
  610.3 18.3 fusion.49
  628.6 132.9 %all-reduce.8.cloned.1.call-done = f32[1024,2048]{1,0:T(8,128)} async-done(((f32[1024,2048]{1,0:T(8,128)}), f32[1024,2048]{1,0:T(8,128)}) %all-reduce.8.cloned.1.call-update) | async-done | bytes 8388624 | tf_op jit(solution)/shard_map/psum | solution.py:70
  790.7 12.6 multiply_reduce_fusion
  803.3 12.1 multiply_convert_fusion
  844.9 278.3 %all-reduce.10.cloned.1.call-done = (f32[1024,2048]{1,0:T(8,128)}, f32[1024,2048]{1,0:T(8,128)}) async-done(((f32[1024,2048]{1,0:T(8,128)}, f32[1024,2048]{1,0:T(8,128)}), (f32[1024,2048]{1,0:T(8,128)}, f32[1024,2048]{1,0:T(8,128)})) %all-reduce.10.cloned.1.call-update) | async-done | bytes 16777232 | tf_op jit(solution)/shard_map/psum | solution.py:70
  1146.7 13.6 fusion.36
  1161.0 16.4 fusion.50
  1177.7 17.1 fusion.27
  1195.5 37.8 %all-reduce = (f32[2,512]{1,0:T(2,128)S(1)}, f32[2048]{0:T(1024)S(1)}) all-reduce(f32[2,512]{1,0:T(2,128)S(1)} %convert_reduce_fusion.2, f32[2048]{0:T(1024)S(1)} %copy-done.48), channel_id=1, replica_groups=mesh['dp'=8,'mp'=4] {'dp'}, use_global_device_ids=true, to_apply=%region_28.29 | all-reduce | flops 3072 | bytes 24576 | tf_op jit(solution)/shard_map/psum | solution.py:231
  1239.6 41.7 %reduce-scatter.6.cloned.1.call-done = f32[256,6]{0,1:T(8,128)} async-done(((f32[2048,6]{0,1:T(8,128)}), f32[256,6]{0,1:T(8,128)}) %reduce-scatter.6.cloned.1.call-update) | async-done | bytes 6160 | tf_op jit(solution)/shard_map/reduce_scatter | solution.py:229
  1283.9 208.1 %reduce-scatter.8.cloned.1.call-done = f32[256,3,512]{2,0,1:T(8,128)} async-done(((f32[2048,3,512]{2,0,1:T(8,128)}), f32[256,3,512]{2,0,1:T(8,128)}) %reduce-scatter.8.cloned.1.call-update) | async-done | bytes 1572880 | tf_op jit(solution)/shard_map/reduce_scatter | solution.py:225
  1496.3 280.9 %reduce-scatter.12.cloned.1.call-done = f32[256,2048]{1,0:T(8,128)} async-done(((f32[2048,2048]{1,0:T(8,128)}), f32[256,2048]{1,0:T(8,128)}) %reduce-scatter.12.cloned.1.call-update) | async-done | bytes 2097168 | tf_op jit(solution)/shard_map/reduce_scatter | solution.py:227
  1781.3 281.4 %reduce-scatter.14.cloned.1.call-done = f32[256,2048]{1,0:T(8,128)} async-done(((f32[2048,2048]{1,0:T(8,128)}), f32[256,2048]{1,0:T(8,128)}) %reduce-scatter.14.cloned.1.call-update) | async-done | bytes 2097168 | tf_op jit(solution)/shard_map/reduce_scatter | solution.py:228
  2077.0 39.2 %psum.63 = f32[]{:T(128)} all-reduce(f32[]{:T(128)S(6)} %add.249), channel_id=1, replica_groups=mesh['dp'=8,'mp'=4] {'dp','mp'}, use_global_device_ids=true, to_apply=%region_41.42 | all-reduce | flops 1 | bytes 8 | tf_op jit(solution)/shard_map/psum | solution.py:249
  (214 shorter events, 205.2 us)
Async XLA Ops:
  7.2 106.5 %all-gather.5.cloned.1.call-start = ((), (), s32[]{:S(2)}) async-start(), calls=%async_computation.5 | async-start | bytes 7077888 | tf_op jit(solution)/shard_map/all_gather | solution.py:92
  9.9 154.1 %all-gather.7.cloned.1.call-start = ((), (), s32[]{:S(2)}) async-start(), calls=%async_computation.6 | async-start | bytes 2359296 | tf_op jit(solution)/shard_map/all_gather | solution.py:93
  11.7 311.2 %all-reduce.6.cloned.1.call-start = ((), (), s32[]{:S(2)}) async-start(), calls=%async_computation.7 | async-start | bytes 16777216 | tf_op jit(solution)/shard_map/psum | solution.py:70
  15.6 109.2 %copy-start.28 = (f32[1024]{0:T(1024)}, f32[1024]{0:T(1024)S(1)}, u32[]{:S(2)}) copy-start(f32[1024]{0:T(1024)S(1)} %broadcast_multiply_fusion.8) | copy-start | bytes 12292
  19.0 105.8 %copy-start.32 = (f32[1024]{0:T(1024)}, f32[1024]{0:T(1024)S(1)}, u32[]{:S(2)}) copy-start(f32[1024]{0:T(1024)S(1)} %fusion.15) | copy-start | bytes 12292
  19.1 105.8 %copy-start.30 = (f32[1024]{0:T(1024)}, f32[1024]{0:T(1024)S(1)}, u32[]{:S(2)}) copy-start(f32[1024]{0:T(1024)S(1)} %fusion.42) | copy-start | bytes 12292
  52.6 72.3 %copy-start.26 = (f32[2048,1]{0,1:T(1,128)}, f32[2048,1]{0,1:T(1,128)S(1)}, u32[]{:S(2)}) copy-start(f32[2048,1]{0,1:T(1,128)S(1)} %get-tuple-element.123) | copy-start | bytes 24580
  52.6 72.3 %copy-start.46 = (f32[2048,1]{0,1:T(1,128)}, f32[2048,1]{0,1:T(1,128)S(1)}, u32[]{:S(2)}) copy-start(f32[2048,1]{0,1:T(1,128)S(1)} %get-tuple-element.124) | copy-start | bytes 24580
  52.6 398.0 %copy-start.44 = (f32[2048,1]{0,1:T(1,128)}, f32[2048,1]{0,1:T(1,128)S(1)}, u32[]{:S(2)}) copy-start(f32[2048,1]{0,1:T(1,128)S(1)} %get-tuple-element.121) | copy-start | bytes 24580
  171.4 279.2 %all-gather.9.cloned.1.call-start = ((), (), s32[]{:S(2)}) async-start(), calls=%async_computation.8 | async-start | bytes 9437184 | tf_op jit(solution)/shard_map/all_gather | solution.py:94
  174.2 402.1 %all-gather.11.cloned.1.call-start = ((), (), s32[]{:S(2)}) async-start(), calls=%async_computation.9 | async-start | bytes 9437184 | tf_op jit(solution)/shard_map/all_gather | solution.py:95
  177.5 584.0 %all-reduce.8.cloned.1.call-start = ((), (), s32[]{:S(2)}) async-start(), calls=%async_computation.10 | async-start | bytes 16777216 | tf_op jit(solution)/shard_map/psum | solution.py:70
  450.6 125.7 %copy-start.49 = (f32[2048]{0:T(1024)S(1)}, f32[2048]{0:T(1024)}, u32[]{:S(2)}) copy-start(f32[2048]{0:T(1024)} %param.35) | copy-start | bytes 24580
  610.3 513.0 %all-reduce.10.cloned.1.call-start = ((), (), s32[]{:S(2)}) async-start(), calls=%async_computation.16 | async-start | bytes 33554432 | tf_op jit(solution)/shard_map/psum | solution.py:70
  834.1 289.2 %copy-start.27 = (f32[2048,1]{0,1:T(1,128)S(1)}, f32[2048,1]{0,1:T(1,128)}, u32[]{:S(2)}) copy-start(f32[2048,1]{0,1:T(1,128)} %copy-done.26) | copy-start | bytes 24580
  834.1 289.1 %copy-start.29 = (f32[1024]{0:T(1024)S(1)}, f32[1024]{0:T(1024)}, u32[]{:S(2)}) copy-start(f32[1024]{0:T(1024)} %copy-done.28) | copy-start | bytes 12292
  834.1 403.0 %reduce-scatter.10.cloned.1.call-start = ((), (), s32[]{:S(2)}) async-start(), calls=%async_computation.13 | async-start | bytes 4718592 | tf_op jit(solution)/shard_map/reduce_scatter | solution.py:226
  844.8 284.8 %copy-start.33 = (f32[1024]{0:T(1024)S(1)}, f32[1024]{0:T(1024)}, u32[]{:S(2)}) copy-start(f32[1024]{0:T(1024)} %copy-done.32) | copy-start | bytes 12292
  844.8 284.8 %copy-start.31 = (f32[1024]{0:T(1024)S(1)}, f32[1024]{0:T(1024)}, u32[]{:S(2)}) copy-start(f32[1024]{0:T(1024)} %copy-done.30) | copy-start | bytes 12292
  844.9 436.4 %reduce-scatter.6.cloned.1.call-start = ((), (), s32[]{:S(2)}) async-start(), calls=%async_computation.11 | async-start | bytes 73728 | tf_op jit(solution)/shard_map/reduce_scatter | solution.py:229
  1146.5 345.5 %reduce-scatter.8.cloned.1.call-start = ((), (), s32[]{:S(2)}) async-start(), calls=%async_computation.12 | async-start | bytes 14155776 | tf_op jit(solution)/shard_map/reduce_scatter | solution.py:225
  1160.3 616.9 %reduce-scatter.12.cloned.1.call-start = ((), (), s32[]{:S(2)}) async-start(), calls=%async_computation.14 | async-start | bytes 18874368 | tf_op jit(solution)/shard_map/reduce_scatter | solution.py:227
  1177.4 885.3 %reduce-scatter.14.cloned.1.call-start = ((), (), s32[]{:S(2)}) async-start(), calls=%async_computation.15 | async-start | bytes 18874368 | tf_op jit(solution)/shard_map/reduce_scatter | solution.py:228
  1194.8 871.9 %copy-start.34 = (f32[2048,1]{0,1:T(1,128)S(1)}, f32[2048,1]{0,1:T(1,128)}, u32[]{:S(2)}) copy-start(f32[2048,1]{0,1:T(1,128)} %get-tuple-element.119) | copy-start | bytes 24580
  (47 other events, 938.4 us)
Sparse Core Ops, SparseCore 0:
  10.7 102.9 all-gather.4
  116.4 47.5 all-gather.6
  171.5 151.3 all-reduce.5
  325.5 125.0 all-gather.8
  453.1 123.1 all-gather.10
  610.4 151.0 all-reduce.7
  834.2 288.9 all-reduce.9
  1127.5 88.2 reduce-scatter.9
  1220.1 61.1 reduce-scatter.5
  1285.1 206.7 reduce-scatter.7
  1496.2 280.9 reduce-scatter.11
  1780.9 281.7 reduce-scatter.13
where the time goes:
time: 2160 us; the launch traced here: 2150 us
  waiting for transfers between devices  1660 us (77%)
  matrix products  195 us (9%)
  other arithmetic  128 us (6%)
  blocking collectives  128 us (6%)
  between operations  23.6 us (1%)
    psum x3, waiting for transfers between devices, sum_over_mp(): summed = lax.psum(term_fn(0, row_count), 'mp')  533 us
    reduce_scatter x1, waiting for transfers between devices, local(): lax.psum_scatter(down_sum, 'dp', scatter_dimension=0, tiled=True)  281 us
    reduce_scatter x1, waiting for transfers between devices, local(): lax.psum_scatter(fc_sum, 'dp', scatter_dimension=0, tiled=True)  281 us
    reduce_scatter x1, waiting for transfers between devices, local(): lax.psum_scatter(qkv_sum, 'dp', scatter_dimension=0, tiled=True)  208 us
    all_gather x1, waiting for transfers between devices, local(): lax.all_gather(low_fc, 'dp', axis=0, tiled=True)  118 us
    all_gather x1, waiting for transfers between devices, local(): lax.all_gather(low_down, 'dp', axis=0, tiled=True)  110 us
    all_gather x1, waiting for transfers between devices, local(): lax.all_gather(low_qkv, 'dp', axis=0, tiled=True)  61 us
  transfers between devices with their start and end apart: 12, of which 11 were waited for; matrix products, arithmetic and copies ran while one was open for 8% of the time, Pallas kernels for 0%

commit v1 on v0

--- a/solution.py
+++ b/solution.py
@@ -67,7 +67,7 @@
     dp_count = lax.axis_size("dp")
 
     def sum_over_mp(term_fn):
-        summed = lax.psum(term_fn(0, row_count), "mp")
+        summed = jnp.sum(lax.all_gather(term_fn(0, row_count), "mp"), axis=0)
         return summed
 
     family_ids = jnp.arange(family_count, dtype=jnp.int32)

time: 2160 us -> 2270 us (1.051)
  other arithmetic: 128 us -> 218 us
    all_gather x0 -> x4, waiting for transfers between devices: none -> 684 us  [sum_over_mp(): summed = jnp.sum(lax.all_gather(term_fn(0, row_count), 'mp'), axis=0)]
    psum x3 -> x0, waiting for transfers between devices: 533 us -> none  [sum_over_mp(): summed = lax.psum(term_fn(0, row_count), 'mp')]
    reduce_scatter x1, waiting for transfers between devices: 281 us -> 157 us  [local(): lax.psum_scatter(fc_sum, 'dp', scatter_dimension=0, tiled=True)]
    reduce_sum x0 -> x4, other arithmetic: none -> 71.5 us  [sum_over_mp(): summed = jnp.sum(lax.all_gather(term_fn(0, row_count), 'mp'), axis=0)]
    reduce_scatter x1, waiting for transfers between devices: 208 us -> 158 us  [local(): lax.psum_scatter(qkv_sum, 'dp', scatter_dimension=0, tiled=True)]
    reduce_scatter x1, waiting for transfers between devices: 0.02 us -> 32.9 us  [local(): lax.psum_scatter(proj_sum, 'dp', scatter_dimension=0, tiled=True)]
    reduce_sum x3 -> x5, other arithmetic: 17.7 us -> 43.3 us  [layer_norm(): return centred * lax.rsqrt(spread + EPS) * gain + shift]
  transfers between devices with their start and end apart: 12 -> 13, of which waited for: 11 -> 13; matrix products, arithmetic and copies ran while one was open for 8% -> 16% of each run, Pallas kernels for 0% -> 0%
where the time goes in v1:
time: 2270 us
  waiting for transfers between devices  1670 us (74%)
  other arithmetic  218 us (10%)
  matrix products  202 us (9%)
  blocking collectives  129 us (6%)
  local copies, waits for them, and re-layouts  26.1 us (1%)
  between operations  23.4 us (1%)
    all_gather x4, waiting for transfers between devices, sum_over_mp(): summed = jnp.sum(lax.all_gather(term_fn(0, row_count), 'mp'), axis=0)  684 us
    reduce_scatter x1, waiting for transfers between devices, local(): lax.psum_scatter(down_sum, 'dp', scatter_dimension=0, tiled=True)  283 us
    reduce_scatter x1, waiting for transfers between devices, local(): lax.psum_scatter(qkv_sum, 'dp', scatter_dimension=0, tiled=True)  158 us
    reduce_scatter x1, waiting for transfers between devices, local(): lax.psum_scatter(fc_sum, 'dp', scatter_dimension=0, tiled=True)  157 us
    all_gather x1, waiting for transfers between devices, local(): lax.all_gather(low_down, 'dp', axis=0, tiled=True)  110 us
    all_gather x1, waiting for transfers between devices, local(): lax.all_gather(low_fc, 'dp', axis=0, tiled=True)  100 us
    reduce_sum x4, other arithmetic, sum_over_mp(): summed = jnp.sum(lax.all_gather(term_fn(0, row_count), 'mp'), axis=0)  71.5 us
    reduce_scatter x1, waiting for transfers between devices, local(): lax.psum_scatter(norm_part, 'dp', scatter_dimension=0, tiled=True)  61.7 us
  transfers between devices with their start and end apart: 13, of which 13 were waited for; matrix products, arithmetic and copies ran while one was open for 16% of the time, Pallas kernels for 0%

profile of v1, /device:TPU:0, one launch (start us, length us, event | category | flops | bytes accessed | tf_op | source)
XLA Modules:
  0.0 2269.3 jit_solution(2571759897764088357)
XLA Ops:
  19.1 32.9 %all_gather.39 = bf16[2048,6]{0,1:T(8,128)(2,1)S(1)} all-gather(bf16[256,6]{0,1:T(8,128)(2,1)S(1)} %convert_element_type.108), channel_id=1, replica_groups=mesh['dp'=8,'mp'=4] {'dp'}, dimensions={0}, use_global_device_ids=true | all-gather | bytes 27648 | tf_op jit(solution)/shard_map/all_gather | solution.py:96
  52.8 60.9 %all-gather.13.cloned.1.call-done = bf16[2048,3,512]{0,2,1:T(8,128)(2,1)} async-done(((bf16[256,3,512]{0,2,1:T(8,128)(2,1)}), bf16[2048,3,512]{0,2,1:T(8,128)(2,1)}) %all-gather.13.cloned.1.call-update) | async-done | bytes 6291472 | tf_op jit(solution)/shard_map/all_gather | solution.py:92
  140.5 23.4 %all-gather.15.cloned.1.call-done = bf16[2048,512]{1,0:T(8,128)(2,1)} async-done(((bf16[256,512]{1,0:T(8,128)(2,1)}), bf16[2048,512]{1,0:T(8,128)(2,1)}) %all-gather.15.cloned.1.call-update) | async-done | bytes 2097168 | tf_op jit(solution)/shard_map/all_gather | solution.py:93
  175.5 196.1 %all-gather.21.cloned.1.call-done = f32[4096,2048]{1,0:T(8,128)} async-done(((f32[1024,2048]{1,0:T(8,128)}), f32[4096,2048]{1,0:T(8,128)}) %all-gather.21.cloned.1.call-update) | async-done | bytes 33554448 | tf_op jit(solution)/shard_map/all_gather | solution.py:70
  399.1 100.1 %all-gather.17.cloned.1.call-done = bf16[2048,2048]{1,0:T(8,128)(2,1)} async-done(((bf16[256,2048]{1,0:T(8,128)(2,1)}), bf16[2048,2048]{1,0:T(8,128)(2,1)}) %all-gather.17.cloned.1.call-update) | async-done | bytes 8388624 | tf_op jit(solution)/shard_map/all_gather | solution.py:94
  514.9 109.9 %all-gather.19.cloned.1.call-done = bf16[2048,2048]{1,0:T(8,128)(2,1)} async-done(((bf16[256,2048]{1,0:T(8,128)(2,1)}), bf16[2048,2048]{1,0:T(8,128)(2,1)}) %all-gather.19.cloned.1.call-update) | async-done | bytes 8388624 | tf_op jit(solution)/shard_map/all_gather | solution.py:95
  624.9 17.3 fusion.49
  643.5 18.8 psum.28
  666.1 21.4 convert_reduce_fusion.1
  702.8 16.8 fusion.50
  719.7 16.9 fusion.27
  736.6 105.4 %all-gather.23.cloned.1.call-done = f32[4096,2048]{1,0:T(8,128)} async-done(((f32[1024,2048]{1,0:T(8,128)}), f32[4096,2048]{1,0:T(8,128)}) %all-gather.23.cloned.1.call-update) | async-done | bytes 33554448 | tf_op jit(solution)/shard_map/all_gather | solution.py:70
  842.0 21.1 reduce_sum.296
  863.1 182.1 %all-gather.25.cloned.1.call-done = f32[4096,2048]{1,0:T(8,128)} async-done(((f32[1024,2048]{1,0:T(8,128)}), f32[4096,2048]{1,0:T(8,128)}) %all-gather.25.cloned.1.call-update) | async-done | bytes 33554448 | tf_op jit(solution)/shard_map/all_gather | solution.py:70
  1045.1 16.7 reduce_sum.344
  1174.7 157.0 %reduce-scatter.12.cloned.1.call-done = f32[256,2048]{1,0:T(8,128)} async-done(((f32[2048,2048]{1,0:T(8,128)}), f32[256,2048]{1,0:T(8,128)}) %reduce-scatter.12.cloned.1.call-update) | async-done | bytes 2097168 | tf_op jit(solution)/shard_map/reduce_scatter | solution.py:227
  1335.1 282.7 %reduce-scatter.14.cloned.1.call-done = f32[256,2048]{1,0:T(8,128)} async-done(((f32[2048,2048]{1,0:T(8,128)}), f32[256,2048]{1,0:T(8,128)}) %reduce-scatter.14.cloned.1.call-update) | async-done | bytes 2097168 | tf_op jit(solution)/shard_map/reduce_scatter | solution.py:228
  1621.8 36.9 %all-reduce = (f32[2,512]{1,0:T(2,128)S(1)}, f32[2048]{0:T(1024)S(1)}) all-reduce(f32[2,512]{1,0:T(2,128)S(1)} %convert_reduce_fusion.2, f32[2048]{0:T(1024)S(1)} %copy-done.54), channel_id=1, replica_groups=mesh['dp'=8,'mp'=4] {'dp'}, use_global_device_ids=true, to_apply=%region_28.29 | all-reduce | flops 3072 | bytes 24576 | tf_op jit(solution)/shard_map/psum | solution.py:231
  1675.9 32.9 %reduce-scatter.10.cloned.1.call-done = f32[256,512]{1,0:T(8,128)} async-done(((f32[2048,512]{1,0:T(8,128)}), f32[256,512]{1,0:T(8,128)}) %reduce-scatter.10.cloned.1.call-update) | async-done | bytes 524304 | tf_op jit(solution)/shard_map/reduce_scatter | solution.py:226
  1711.2 200.5 %all-gather.27.cloned.1.call-done = f32[4096,2048]{1,0:T(8,128)} async-done(((f32[1024,2048]{1,0:T(8,128)}), f32[4096,2048]{1,0:T(8,128)}) %all-gather.27.cloned.1.call-update) | async-done | bytes 33554448 | tf_op jit(solution)/shard_map/all_gather | solution.py:70
  1911.7 17.0 reduce_sum.348
  1965.4 158.0 %reduce-scatter.8.cloned.1.call-done = f32[256,3,512]{2,0,1:T(8,128)} async-done(((f32[2048,3,512]{2,0,1:T(8,128)}), f32[256,3,512]{2,0,1:T(8,128)}) %reduce-scatter.8.cloned.1.call-update) | async-done | bytes 1572880 | tf_op jit(solution)/shard_map/reduce_scatter | solution.py:225
  2126.4 61.7 %reduce-scatter.6.cloned.1.call-done = f32[256,6]{0,1:T(8,128)} async-done(((f32[2048,6]{0,1:T(8,128)}), f32[256,6]{0,1:T(8,128)}) %reduce-scatter.6.cloned.1.call-update) | async-done | bytes 6160 | tf_op jit(solution)/shard_map/reduce_scatter | solution.py:229
  2193.3 40.4 %psum.31 = f32[]{:T(128)} all-reduce(f32[]{:T(128)S(6)} %add.241), channel_id=1, replica_groups=mesh['dp'=8,'mp'=4] {'dp','mp'}, use_global_device_ids=true, to_apply=%region_41.42 | all-reduce | flops 1 | bytes 8 | tf_op jit(solution)/shard_map/psum | solution.py:249
  (232 shorter events, 319.3 us)
Async XLA Ops:
  7.2 106.5 %all-gather.13.cloned.1.call-start = ((), (), s32[]{:S(2)}) async-start(), calls=%async_computation.5 | async-start | bytes 7077888 | tf_op jit(solution)/shard_map/all_gather | solution.py:92
  9.9 154.1 %all-gather.15.cloned.1.call-start = ((), (), s32[]{:S(2)}) async-start(), calls=%async_computation.6 | async-start | bytes 2359296 | tf_op jit(solution)/shard_map/all_gather | solution.py:93
  11.7 359.9 %all-gather.21.cloned.1.call-start = ((), (), s32[]{:S(2)}) async-start(), calls=%async_computation.14 | async-start | bytes 41943040 | tf_op jit(solution)/shard_map/all_gather | solution.py:70
  171.5 327.7 %all-gather.17.cloned.1.call-start = ((), (), s32[]{:S(2)}) async-start(), calls=%async_computation.7 | async-start | bytes 9437184 | tf_op jit(solution)/shard_map/all_gather | solution.py:94
  172.7 452.2 %all-gather.19.cloned.1.call-start = ((), (), s32[]{:S(2)}) async-start(), calls=%async_computation.8 | async-start | bytes 9437184 | tf_op jit(solution)/shard_map/all_gather | solution.py:95
  175.5 666.5 %all-gather.23.cloned.1.call-start = ((), (), s32[]{:S(2)}) async-start(), calls=%async_computation.15 | async-start | bytes 41943040 | tf_op jit(solution)/shard_map/all_gather | solution.py:70
  642.2 403.0 %all-gather.25.cloned.1.call-start = ((), (), s32[]{:S(2)}) async-start(), calls=%async_computation.16 | async-start | bytes 41943040 | tf_op jit(solution)/shard_map/all_gather | solution.py:70
  702.8 628.9 %reduce-scatter.12.cloned.1.call-start = ((), (), s32[]{:S(2)}) async-start(), calls=%async_computation.12 | async-start | bytes 18874368 | tf_op jit(solution)/shard_map/reduce_scatter | solution.py:227
  719.6 898.1 %reduce-scatter.14.cloned.1.call-start = ((), (), s32[]{:S(2)}) async-start(), calls=%async_computation.13 | async-start | bytes 18874368 | tf_op jit(solution)/shard_map/reduce_scatter | solution.py:228
  736.6 972.1 %reduce-scatter.10.cloned.1.call-start = ((), (), s32[]{:S(2)}) async-start(), calls=%async_computation.11 | async-start | bytes 4718592 | tf_op jit(solution)/shard_map/reduce_scatter | solution.py:226
  1090.3 821.4 %all-gather.27.cloned.1.call-start = ((), (), s32[]{:S(2)}) async-start(), calls=%async_computation.17 | async-start | bytes 41943040 | tf_op jit(solution)/shard_map/all_gather | solution.py:70
  1159.9 963.5 %reduce-scatter.8.cloned.1.call-start = ((), (), s32[]{:S(2)}) async-start(), calls=%async_computation.10 | async-start | bytes 14155776 | tf_op jit(solution)/shard_map/reduce_scatter | solution.py:225
  1174.6 447.2 %copy-start.54 = (f32[2048]{0:T(1024)S(1)}, f32[2048]{0:T(1024)}, u32[]{:S(2)}) copy-start(f32[2048]{0:T(1024)} %get-tuple-element.127) | copy-start | bytes 24580
  1174.6 1013.5 %reduce-scatter.6.cloned.1.call-start = ((), (), s32[]{:S(2)}) async-start(), calls=%async_computation.9 | async-start | bytes 73728 | tf_op jit(solution)/shard_map/reduce_scatter | solution.py:229
  1954.3 281.6 %copy-start.49 = (f32[2,512]{1,0:T(2,128)S(1)}, f32[2,512]{1,0:T(2,128)}, u32[]{:S(2)}) copy-start(f32[2,512]{1,0:T(2,128)} %param.32) | copy-start | bytes 12292
  1954.3 282.2 %copy-start.59 = (f32[2,512]{1,0:T(2,128)S(1)}, f32[2,512]{1,0:T(2,128)}, u32[]{:S(2)}) copy-start(f32[2,512]{1,0:T(2,128)} %param.46) | copy-start | bytes 12292
  1954.3 282.8 %copy-start.50 = (f32[2048]{0:T(1024)S(1)}, f32[2048]{0:T(1024)}, u32[]{:S(2)}) copy-start(f32[2048]{0:T(1024)} %param.49) | copy-start | bytes 24580
  1954.3 283.3 %copy-start.45 = (f32[256,6]{0,1:T(8,128)S(1)}, f32[256,6]{0,1:T(8,128)}, u32[]{:S(2)}) copy-start(f32[256,6]{0,1:T(8,128)} %param.31) | copy-start | bytes 18436
  1954.3 283.3 %copy-start.58 = (f32[256,6]{0,1:T(8,128)S(1)}, f32[256,6]{0,1:T(8,128)}, u32[]{:S(2)}) copy-start(f32[256,6]{0,1:T(8,128)} %param.38) | copy-start | bytes 18436
  1954.3 285.3 %copy-start.51 = (f32[256,6]{0,1:T(8,128)S(1)}, f32[256,6]{0,1:T(8,128)}, u32[]{:S(2)}) copy-start(f32[256,6]{0,1:T(8,128)} %param.45) | copy-start | bytes 18436
  1954.3 285.9 %copy-start.24 = (f32[256,512]{1,0:T(8,128)S(1)}, f32[256,512]{1,0:T(8,128)}, u32[]{:S(2)}) copy-start(f32[256,512]{1,0:T(8,128)} %param.34) | copy-start | bytes 1572868
  1954.4 285.9 %copy-start.25 = (f32[256,512]{1,0:T(8,128)S(1)}, f32[256,512]{1,0:T(8,128)}, u32[]{:S(2)}) copy-start(f32[256,512]{1,0:T(8,128)} %reduce-scatter.10.cloned.1.call-done) | copy-start | bytes 1572868
  1954.4 285.9 %copy-start.30 = (f32[256,512]{1,0:T(8,128)S(1)}, f32[256,512]{1,0:T(8,128)}, u32[]{:S(2)}) copy-start(f32[256,512]{1,0:T(8,128)} %param.41) | copy-start | bytes 1572868
  1954.4 289.9 %copy-start.16 = (f32[256,3,512]{2,0,1:T(8,128)S(1)}, f32[256,3,512]{2,0,1:T(8,128)}, u32[]{:S(2)}) copy-start(f32[256,3,512]{2,0,1:T(8,128)} %param.33) | copy-start | bytes 4718596
  (53 other events, 1900.8 us)
Sparse Core Ops, SparseCore 0:
  10.7 102.9 all-gather.12
  116.4 47.4 all-gather.14
  171.6 199.9 all-gather.20
  374.2 124.9 all-gather.16
  501.7 123.1 all-gather.18
  642.3 199.6 all-gather.22
  843.6 201.5 all-gather.24
  1048.9 282.7 reduce-scatter.11
  1336.0 281.7 reduce-scatter.13
  1621.2 87.4 reduce-scatter.9
  1710.4 201.2 all-gather.26
  1915.6 207.7 reduce-scatter.7
  2127.7 60.3 reduce-scatter.5
